TPU v7x, 32 devices: a whole 2x2x4 slice. The times are simulated.
32 devices in a mesh: group: 4 (over y, core), member: 8 (over z, x).
Axes of the slice: x: 2, y: 2, z: 4, core: 2. Of those that a mesh axis runs over, the one named last changes fastest.
Arguments:
- features: bfloat16 [16384, 128], P(('group', 'member')), may hold values from -6 to 6
- edge_tiles: bfloat16 [8192, 128, 128], P(('group', 'member')), may hold values from -0.09375 to 0.09375
- tile_slot: int32 [32, 256], P(('group', 'member')), may hold values from 0 to 7
- tile_column: int32 [32, 256], P(('group', 'member')), may hold values from 0 to 31
- mirror_count: int32 [32, 4], P(('group', 'member')), may hold values from 0 to 2, as said below
- mirror_block: int32 [32, 4, 2], P(('group', 'member')), may hold values from 0 to 3, as said below
- weight_first: bfloat16 [128, 256], replicated, may hold values from -0.5 to 0.5
- bias_first: float32 [256], replicated, may hold values from -3 to 3
- weight_second: bfloat16 [256, 256], replicated, may hold values from -0.375 to 0.375
- bias_second: float32 [256], replicated, may hold values from -3 to 3
Outputs:
- layer_out: bfloat16 [16384, 256], P(('group', 'member'))
Inputs may be any that keep to these rules, and one draw needn't show every extreme that they name: `mirror_count`: at most 2 live mirror slots of one device for one destination group. `mirror_block`: the 2 entries of one device and destination group are distinct.
All inputs are finite; a program needn't handle non-finite values.
Results may differ from a plain program's by a relative error of at most 0.01.
Values may be sent and summed in bfloat16 or wider, within the bound.
A program may use at most 64 MiB of HBM per device.

v0:
```python
import math
import jax
import jax.numpy as jnp
from jax import lax
from jax.sharding import PartitionSpec as P


def expand(owners, block_count):
    return (owners[..., None] == jnp.arange(block_count)[None, None, :]).astype(jnp.bfloat16)


def fold_tiles(sources, edge_tiles, slot_ids, column_ids, alive_mask, slot_total):
    tile_total = edge_tiles.shape[0]
    tile_size = edge_tiles.shape[1]
    channels = sources.shape[2]
    block_tiles = math.gcd(tile_total, 32)
    rounds = tile_total // block_tiles
    tile_sets = edge_tiles.reshape(rounds, block_tiles, tile_size, tile_size)
    slot_sets = slot_ids.reshape(rounds, block_tiles)
    column_sets = column_ids.reshape(rounds, block_tiles)
    alive_sets = alive_mask.astype(jnp.float32).reshape(rounds, block_tiles)

    def advance(totals, pieces):
        tile_set, column_set, slot_set, alive_set = pieces
        source = jnp.take(sources, column_set, axis=0)
        products = jnp.einsum("tij,tjf->tif", tile_set, source, preferred_element_type=jnp.float32)
        return (totals.at[slot_set].add(products * alive_set[:, None, None]), None)

    start = jnp.zeros((slot_total, tile_size, channels), jnp.float32)
    totals, _ = lax.scan(advance, start, (tile_sets, column_sets, slot_sets, alive_sets))
    return totals.astype(jnp.bfloat16)


def body(
    features,
    edge_tiles,
    tile_slot,
    tile_column,
    mirror_count,
    mirror_block,
    weight_first,
    bias_first,
    weight_second,
    bias_second,
):
    group_count = lax.axis_size("group")
    slot_room = mirror_block.shape[2]
    tile_size = edge_tiles.shape[1]
    block_count = features.shape[0] // tile_size
    slot_ids = tile_slot[0]
    column_ids = tile_column[0]
    counts = mirror_count[0]
    targets = mirror_block[0]
    dest_group = slot_ids // slot_room
    within = slot_ids % slot_room
    count_of = jnp.sum(
        jnp.where(dest_group[:, None] == jnp.arange(group_count)[None, :], counts[None, :], 0),
        axis=1,
    )
    alive_mask = within < count_of
    spread = expand(targets, block_count)
    slot_total = group_count * slot_room

    def reduce_rows(partials):
        channels = partials.shape[2]
        spread_sums = jnp.einsum(
            "gcb,gcif->gbif",
            spread,
            partials.reshape(group_count, slot_room, tile_size, channels),
            preferred_element_type=jnp.float32,
        )
        return lax.psum_scatter(
            spread_sums.reshape(group_count * block_count, tile_size, channels).astype(
                jnp.bfloat16
            ),
            "group",
            scatter_dimension=0,
            tiled=True,
        ).astype(jnp.float32)

    local_rows = features.reshape(block_count, tile_size, features.shape[1])
    gathered = lax.all_gather(local_rows, "member", axis=0, tiled=True)
    first_sum = reduce_rows(
        fold_tiles(gathered, edge_tiles, slot_ids, column_ids, alive_mask, slot_total)
    ).astype(jnp.bfloat16)
    flat = first_sum.reshape(-1, first_sum.shape[2])
    result = jnp.maximum(
        jnp.dot(flat, weight_first, preferred_element_type=jnp.float32) + bias_first, 0.0
    )
    hidden = result.astype(jnp.bfloat16).reshape(first_sum.shape[0], tile_size, -1)
    sources = lax.all_gather(hidden, "member", axis=0, tiled=True)
    second = reduce_rows(
        fold_tiles(sources, edge_tiles, slot_ids, column_ids, alive_mask, slot_total)
    ).astype(jnp.bfloat16)
    flat_second = second.reshape(block_count * tile_size, -1)
    return (
        jnp.dot(flat_second, weight_second, preferred_element_type=jnp.float32) + bias_second
    ).astype(jnp.bfloat16)


def solution(mesh):
    placed = (
        P(("group", "member"), None),
        P(("group", "member"), None, None),
        P(("group", "member"), None),
        P(("group", "member"), None),
        P(("group", "member"), None),
        P(("group", "member"), None, None),
        P(),
        P(),
        P(),
        P(),
    )
    return jax.shard_map(
        body, mesh=mesh, in_specs=placed, out_specs=P(("group", "member"), None), check_vma=False
    )
```

profile of v0, /device:TPU:0, one launch (start us, length us, event | category | flops | bytes accessed | tf_op | source)
XLA Modules:
  0.0 324.9 jit_solution(12725843926485415464)
XLA Ops:
  13.1 39.3 %all-gather.3.cloned.1.call-done = bf16[32,128,128]{2,1,0:T(8,128)(2,1)} async-done(((bf16[4,128,128]{2,1,0:T(8,128)(2,1)}), bf16[32,128,128]{2,1,0:T(8,128)(2,1)}) %all-gather.3.cloned.1.call-update) | async-done | bytes 1048592 | tf_op jit(solution)/shard_map/all_gather | solution.py:82
  52.4 62.0 %while.20 = (s32[]{:T(128)}, f32[8,128,128]{2,1,0:T(8,128)S(1)}, s32[8,32]{1,0:T(8,128)S(1)}, bf16[8,32,128,128]{3,2,1,0:T(8,128)(2,1)}, s32[8,32]{1,0:T(8,128)S...) while((s32[]{:T(128)}, f32[8,128,128]{2,1,0:T(8,128)S(1)}, s32[8,32]{1,0:T(8,128)S(1)}, ...), condition=%wide.region_3.4_spmd, body=%wide.region_1.3_spmd.sunk | while | flops 135792000 | bytes 12589089 | solution.py:30
  52.5 2.9 gather_fusion
  60.2 2.9 gather_fusion
  67.9 2.9 gather_fusion
  75.7 2.9 gather_fusion
  83.4 2.9 gather_fusion
  88.5 2.7 scatter_fusion
  91.2 2.9 gather_fusion
  98.9 2.9 gather_fusion
  104.0 2.7 scatter_fusion
  106.7 2.9 gather_fusion
  116.0 20.5 %reduce-scatter.3.cloned.1.call-done = bf16[4,128,128]{2,1,0:T(8,128)(2,1)} async-done(((bf16[16,128,128]{2,1,0:T(8,128)(2,1)}), bf16[4,128,128]{2,1,0:T(8,128)(2,1)}) %reduce-scatter.3.cloned.1.call-update) | async-done | bytes 131088 | tf_op jit(solution)/shard_map/reduce_scatter | solution.py:72
  138.4 49.8 %all-gather.5.cloned.1.call-done = bf16[32,128,256]{2,1,0:T(8,128)(2,1)} async-done(((bf16[4,128,256]{2,1,0:T(8,128)(2,1)}), bf16[32,128,256]{2,1,0:T(8,128)(2,1)}) %all-gather.5.cloned.1.call-update) | async-done | bytes 2097168 | tf_op jit(solution)/shard_map/all_gather | solution.py:91
  188.3 102.1 %while.21 = (s32[]{:T(128)}, f32[8,128,256]{2,1,0:T(8,128)S(1)}, s32[8,32]{1,0:T(8,128)S(1)}, bf16[8,32,128,128]{3,2,1,0:T(8,128)(2,1)}, s32[8,32]{1,0:T(8,128)S...) while((s32[]{:T(128)}, f32[8,128,256]{2,1,0:T(8,128)S(1)}, s32[8,32]{1,0:T(8,128)S(1)}, ...), condition=%wide.region_7.8_spmd, body=%wide.region_5.7_spmd.sunk | while | flops 271582592 | bytes 24123424 | solution.py:30
  190.7 3.9 %convolution_multiply_fusion.5 = f32[32,128,256]{2,1,0:T(8,128)} fusion(f32[32]{0:T(128)S(1)} %fusion.53, bf16[32,128,256]{2,1,0:T(8,128)(2,1)S(1)} %gather_fusion.1, pred[32]{0:T(512)(128)(4,1)S(1)} %compare_and_fusion.5, bf16[8,32,128,128]{3,2,1,0:T(8,128)(2,1)} %get-tuple-element.250, s32[]{:T(128)} %get-tuple-element.239), kind=kOutput, calls=%fused_computation.24.clone.1 | convolution fusion | flops 270532608 | bytes 7340704 | tf_op jit(solution)/shard_map/while/body/eval_jaxpr/tij,tjf->tif/dot_general | solution.py:26
  194.6 6.4 %scatter_fusion.1 = f32[8,128,256]{2,1,0:T(8,128)S(1)} fusion(f32[8,128,256]{2,1,0:T(8,128)S(1)} %get-tuple-element.240, s32[32]{0:T(128)S(1)} %get-tuple-element.205, f32[32,128,256]{2,1,0:T(8,128)} %convolution_multiply_fusion.5), kind=kCustom, calls=%fused_computation.3.clone.1 | custom fusion | flops 1048576 | bytes 12583040 | tf_op jit(solution)/shard_map/while/body/eval_jaxpr/scatter-add | solution.py:27
  203.4 3.9 %convolution_multiply_fusion.5 = f32[32,128,256]{2,1,0:T(8,128)} fusion(f32[32]{0:T(128)S(1)} %fusion.53, bf16[32,128,256]{2,1,0:T(8,128)(2,1)S(1)} %gather_fusion.1, pred[32]{0:T(512)(128)(4,1)S(1)} %compare_and_fusion.5, bf16[8,32,128,128]{3,2,1,0:T(8,128)(2,1)} %get-tuple-element.250, s32[]{:T(128)} %get-tuple-element.239), kind=kOutput, calls=%fused_computation.24.clone.1 | convolution fusion | flops 270532608 | bytes 7340704 | tf_op jit(solution)/shard_map/while/body/eval_jaxpr/tij,tjf->tif/dot_general | solution.py:26
  207.3 6.4 %scatter_fusion.1 = f32[8,128,256]{2,1,0:T(8,128)S(1)} fusion(f32[8,128,256]{2,1,0:T(8,128)S(1)} %get-tuple-element.240, s32[32]{0:T(128)S(1)} %get-tuple-element.205, f32[32,128,256]{2,1,0:T(8,128)} %convolution_multiply_fusion.5), kind=kCustom, calls=%fused_computation.3.clone.1 | custom fusion | flops 1048576 | bytes 12583040 | tf_op jit(solution)/shard_map/while/body/eval_jaxpr/scatter-add | solution.py:27
  216.2 3.9 %convolution_multiply_fusion.5 = f32[32,128,256]{2,1,0:T(8,128)} fusion(f32[32]{0:T(128)S(1)} %fusion.53, bf16[32,128,256]{2,1,0:T(8,128)(2,1)S(1)} %gather_fusion.1, pred[32]{0:T(512)(128)(4,1)S(1)} %compare_and_fusion.5, bf16[8,32,128,128]{3,2,1,0:T(8,128)(2,1)} %get-tuple-element.250, s32[]{:T(128)} %get-tuple-element.239), kind=kOutput, calls=%fused_computation.24.clone.1 | convolution fusion | flops 270532608 | bytes 7340704 | tf_op jit(solution)/shard_map/while/body/eval_jaxpr/tij,tjf->tif/dot_general | solution.py:26
  220.1 6.5 %scatter_fusion.1 = f32[8,128,256]{2,1,0:T(8,128)S(1)} fusion(f32[8,128,256]{2,1,0:T(8,128)S(1)} %get-tuple-element.240, s32[32]{0:T(128)S(1)} %get-tuple-element.205, f32[32,128,256]{2,1,0:T(8,128)} %convolution_multiply_fusion.5), kind=kCustom, calls=%fused_computation.3.clone.1 | custom fusion | flops 1048576 | bytes 12583040 | tf_op jit(solution)/shard_map/while/body/eval_jaxpr/scatter-add | solution.py:27
  228.9 3.9 %convolution_multiply_fusion.5 = f32[32,128,256]{2,1,0:T(8,128)} fusion(f32[32]{0:T(128)S(1)} %fusion.53, bf16[32,128,256]{2,1,0:T(8,128)(2,1)S(1)} %gather_fusion.1, pred[32]{0:T(512)(128)(4,1)S(1)} %compare_and_fusion.5, bf16[8,32,128,128]{3,2,1,0:T(8,128)(2,1)} %get-tuple-element.250, s32[]{:T(128)} %get-tuple-element.239), kind=kOutput, calls=%fused_computation.24.clone.1 | convolution fusion | flops 270532608 | bytes 7340704 | tf_op jit(solution)/shard_map/while/body/eval_jaxpr/tij,tjf->tif/dot_general | solution.py:26
  232.9 6.5 %scatter_fusion.1 = f32[8,128,256]{2,1,0:T(8,128)S(1)} fusion(f32[8,128,256]{2,1,0:T(8,128)S(1)} %get-tuple-element.240, s32[32]{0:T(128)S(1)} %get-tuple-element.205, f32[32,128,256]{2,1,0:T(8,128)} %convolution_multiply_fusion.5), kind=kCustom, calls=%fused_computation.3.clone.1 | custom fusion | flops 1048576 | bytes 12583040 | tf_op jit(solution)/shard_map/while/body/eval_jaxpr/scatter-add | solution.py:27
  241.7 3.9 %convolution_multiply_fusion.5 = f32[32,128,256]{2,1,0:T(8,128)} fusion(f32[32]{0:T(128)S(1)} %fusion.53, bf16[32,128,256]{2,1,0:T(8,128)(2,1)S(1)} %gather_fusion.1, pred[32]{0:T(512)(128)(4,1)S(1)} %compare_and_fusion.5, bf16[8,32,128,128]{3,2,1,0:T(8,128)(2,1)} %get-tuple-element.250, s32[]{:T(128)} %get-tuple-element.239), kind=kOutput, calls=%fused_computation.24.clone.1 | convolution fusion | flops 270532608 | bytes 7340704 | tf_op jit(solution)/shard_map/while/body/eval_jaxpr/tij,tjf->tif/dot_general | solution.py:26
  245.6 6.4 %scatter_fusion.1 = f32[8,128,256]{2,1,0:T(8,128)S(1)} fusion(f32[8,128,256]{2,1,0:T(8,128)S(1)} %get-tuple-element.240, s32[32]{0:T(128)S(1)} %get-tuple-element.205, f32[32,128,256]{2,1,0:T(8,128)} %convolution_multiply_fusion.5), kind=kCustom, calls=%fused_computation.3.clone.1 | custom fusion | flops 1048576 | bytes 12583040 | tf_op jit(solution)/shard_map/while/body/eval_jaxpr/scatter-add | solution.py:27
  254.4 3.9 %convolution_multiply_fusion.5 = f32[32,128,256]{2,1,0:T(8,128)} fusion(f32[32]{0:T(128)S(1)} %fusion.53, bf16[32,128,256]{2,1,0:T(8,128)(2,1)S(1)} %gather_fusion.1, pred[32]{0:T(512)(128)(4,1)S(1)} %compare_and_fusion.5, bf16[8,32,128,128]{3,2,1,0:T(8,128)(2,1)} %get-tuple-element.250, s32[]{:T(128)} %get-tuple-element.239), kind=kOutput, calls=%fused_computation.24.clone.1 | convolution fusion | flops 270532608 | bytes 7340704 | tf_op jit(solution)/shard_map/while/body/eval_jaxpr/tij,tjf->tif/dot_general | solution.py:26
  258.4 6.4 %scatter_fusion.1 = f32[8,128,256]{2,1,0:T(8,128)S(1)} fusion(f32[8,128,256]{2,1,0:T(8,128)S(1)} %get-tuple-element.240, s32[32]{0:T(128)S(1)} %get-tuple-element.205, f32[32,128,256]{2,1,0:T(8,128)} %convolution_multiply_fusion.5), kind=kCustom, calls=%fused_computation.3.clone.1 | custom fusion | flops 1048576 | bytes 12583040 | tf_op jit(solution)/shard_map/while/body/eval_jaxpr/scatter-add | solution.py:27
  267.2 3.9 %convolution_multiply_fusion.5 = f32[32,128,256]{2,1,0:T(8,128)} fusion(f32[32]{0:T(128)S(1)} %fusion.53, bf16[32,128,256]{2,1,0:T(8,128)(2,1)S(1)} %gather_fusion.1, pred[32]{0:T(512)(128)(4,1)S(1)} %compare_and_fusion.5, bf16[8,32,128,128]{3,2,1,0:T(8,128)(2,1)} %get-tuple-element.250, s32[]{:T(128)} %get-tuple-element.239), kind=kOutput, calls=%fused_computation.24.clone.1 | convolution fusion | flops 270532608 | bytes 7340704 | tf_op jit(solution)/shard_map/while/body/eval_jaxpr/tij,tjf->tif/dot_general | solution.py:26
  271.1 6.5 %scatter_fusion.1 = f32[8,128,256]{2,1,0:T(8,128)S(1)} fusion(f32[8,128,256]{2,1,0:T(8,128)S(1)} %get-tuple-element.240, s32[32]{0:T(128)S(1)} %get-tuple-element.205, f32[32,128,256]{2,1,0:T(8,128)} %convolution_multiply_fusion.5), kind=kCustom, calls=%fused_computation.3.clone.1 | custom fusion | flops 1048576 | bytes 12583040 | tf_op jit(solution)/shard_map/while/body/eval_jaxpr/scatter-add | solution.py:27
  279.9 3.9 %convolution_multiply_fusion.5 = f32[32,128,256]{2,1,0:T(8,128)} fusion(f32[32]{0:T(128)S(1)} %fusion.53, bf16[32,128,256]{2,1,0:T(8,128)(2,1)S(1)} %gather_fusion.1, pred[32]{0:T(512)(128)(4,1)S(1)} %compare_and_fusion.5, bf16[8,32,128,128]{3,2,1,0:T(8,128)(2,1)} %get-tuple-element.250, s32[]{:T(128)} %get-tuple-element.239), kind=kOutput, calls=%fused_computation.24.clone.1 | convolution fusion | flops 270532608 | bytes 7340704 | tf_op jit(solution)/shard_map/while/body/eval_jaxpr/tij,tjf->tif/dot_general | solution.py:26
  283.9 6.5 %scatter_fusion.1 = f32[8,128,256]{2,1,0:T(8,128)S(1)} fusion(f32[8,128,256]{2,1,0:T(8,128)S(1)} %get-tuple-element.240, s32[32]{0:T(128)S(1)} %get-tuple-element.205, f32[32,128,256]{2,1,0:T(8,128)} %convolution_multiply_fusion.5), kind=kCustom, calls=%fused_computation.3.clone.1 | custom fusion | flops 1048576 | bytes 12583040 | tf_op jit(solution)/shard_map/while/body/eval_jaxpr/scatter-add | solution.py:27
  292.9 23.6 %reduce-scatter.5.cloned.1.call-done = bf16[4,128,256]{2,1,0:T(8,128)(2,1)} async-done(((bf16[16,128,256]{2,1,0:T(8,128)(2,1)}), bf16[4,128,256]{2,1,0:T(8,128)(2,1)}) %reduce-scatter.5.cloned.1.call-update) | async-done | bytes 262160 | tf_op jit(solution)/shard_map/reduce_scatter | solution.py:72
  (122 shorter events, 65.7 us)
Async XLA Ops:
  6.5 309.9 %copy-start = (bf16[256,256]{1,0:T(8,128)(2,1)S(1)}, bf16[256,256]{1,0:T(8,128)(2,1)}, u32[]{:S(2)}) copy-start(bf16[256,256]{1,0:T(8,128)(2,1)} %param.22) | copy-start | bytes 393220
  6.5 45.8 %all-gather.3.cloned.1.call-start = ((), (), s32[]{:S(2)}) async-start(), calls=%async_computation.2 | async-start | bytes 1179648 | tf_op jit(solution)/shard_map/all_gather | solution.py:82
  7.3 129.3 %reduce-scatter.3.cloned.1.call-start = ((), (), s32[]{:S(2)}) async-start(), calls=%async_computation.3 | async-start | bytes 655360 | tf_op jit(solution)/shard_map/reduce_scatter | solution.py:72
  114.4 22.2 %copy-start.1 = (bf16[128,256]{1,0:T(8,128)(2,1)S(1)}, bf16[128,256]{1,0:T(8,128)(2,1)}, u32[]{:S(2)}) copy-start(bf16[128,256]{1,0:T(8,128)(2,1)} %param.20) | copy-start | bytes 196612
  114.4 22.1 %copy-start.2 = (f32[256]{0:T(256)S(1)}, f32[256]{0:T(256)}, u32[]{:S(2)}) copy-start(f32[256]{0:T(256)} %param.21) | copy-start | bytes 3076
  116.0 72.2 %all-gather.5.cloned.1.call-start = ((), (), s32[]{:S(2)}) async-start(), calls=%async_computation.4 | async-start | bytes 2359296 | tf_op jit(solution)/shard_map/all_gather | solution.py:91
  138.4 178.1 %reduce-scatter.5.cloned.1.call-start = ((), (), s32[]{:S(2)}) async-start(), calls=%async_computation.5 | async-start | bytes 1310720 | tf_op jit(solution)/shard_map/reduce_scatter | solution.py:72
  291.7 24.8 %copy-start.3 = (f32[256]{0:T(256)S(1)}, f32[256]{0:T(256)}, u32[]{:S(2)}) copy-start(f32[256]{0:T(256)} %param.23) | copy-start | bytes 3076
Sparse Core Ops, SparseCore 0:
  9.5 42.8 all-gather.2
  116.1 20.4 reduce-scatter.2
  138.9 49.2 all-gather.4
  293.0 23.4 reduce-scatter.4
where the time goes:
time: 327 us; the launch traced here: 325 us
  waiting for transfers between devices  134 us (41%)
  other arithmetic  77.7 us (24%)
  matrix products  53.4 us (16%)
  local copies, waits for them, and re-layouts  45.6 us (14%)
  between operations  13.2 us (4%)
    scatter-add x16, other arithmetic, advance(): return (totals.at[slot_set].add(products * alive_set[:, None, None]), None)  72.9 us
    all_gather x1, waiting for transfers between devices, body(): sources = lax.all_gather(hidden, 'member', axis=0, tiled=True)  49.8 us
    dot_general x16, matrix products, advance(): jnp.einsum('tij,tjf->tif', tile_set, source, preferred_element_type=jnp.f...  47.9 us
    reduce_scatter x2, waiting for transfers between devices, reduce_rows(): lax.psum_scatter(spread_sums.reshape(group_count * block_count, tile_size...  44.1 us
    gather x16, local copies, waits for them, and re-layouts, advance(): source = jnp.take(sources, column_set, axis=0)  41.7 us
    all_gather x1, waiting for transfers between devices, body(): gathered = lax.all_gather(local_rows, 'member', axis=0, tiled=True)  39.3 us
  transfers between devices with their start and end apart: 4, of which 4 were waited for; matrix products, arithmetic and copies ran while one was open for 2% of the time, Pallas kernels for 0%

commit v1 on v0

--- a/solution.py
+++ b/solution.py
@@ -3,6 +3,23 @@
 import jax.numpy as jnp
 from jax import lax
 from jax.sharding import PartitionSpec as P
+
+
+def in_order(blocks, dim):
+    blocks = jnp.moveaxis(blocks, 0, dim)
+    shape = blocks.shape
+    return blocks.reshape(*shape[:dim], shape[dim] * shape[dim + 1], *shape[dim + 2 :])
+
+
+def grow_blocks(x, axis):
+    peers, index = (lax.axis_size(axis), lax.axis_index(axis))
+    tiles, apart = (x[None], 1)
+    while apart < peers:
+        other = lax.ppermute(tiles, axis, [(i, i ^ apart) for i in range(peers)])
+        low = index & apart == 0
+        tiles = jnp.concatenate([jnp.where(low, tiles, other), jnp.where(low, other, tiles)])
+        apart *= 2
+    return tiles
 
 
 def expand(owners, block_count):
@@ -88,7 +105,7 @@
         jnp.dot(flat, weight_first, preferred_element_type=jnp.float32) + bias_first, 0.0
     )
     hidden = result.astype(jnp.bfloat16).reshape(first_sum.shape[0], tile_size, -1)
-    sources = lax.all_gather(hidden, "member", axis=0, tiled=True)
+    sources = in_order(grow_blocks(hidden, "member"), 0)
     second = reduce_rows(
         fold_tiles(sources, edge_tiles, slot_ids, column_ids, alive_mask, slot_total)
     ).astype(jnp.bfloat16)

time: 327 us -> 347 us (1.061)
  waiting for transfers between devices: 134 us -> 148 us
  starting transfers between devices: 0.12 us -> 5.62 us
    ppermute x0 -> x3, waiting for transfers between devices: none -> 62 us  [grow_blocks(): other = lax.ppermute(tiles, axis, [(i, i ^ apart) for i in range(peers)])]
    all_gather x1 -> x0, waiting for transfers between devices: 49.8 us -> none  [body(): sources = lax.all_gather(hidden, 'member', axis=0, tiled=True)]
    ppermute x0 -> x3, starting transfers between devices: none -> 5.54 us  [grow_blocks(): other = lax.ppermute(tiles, axis, [(i, i ^ apart) for i in range(peers)])]
  transfers between devices with their start and end apart: 4 -> 6, of which waited for: 4 -> 6; matrix products, arithmetic and copies ran while one was open for 2% -> 2% of each run, Pallas kernels for 0% -> 0%
where the time goes in v1:
time: 347 us; the launch traced here: 345 us
  waiting for transfers between devices  148 us (43%)
  other arithmetic  79.4 us (23%)
  matrix products  52.8 us (15%)
  local copies, waits for them, and re-layouts  45.5 us (13%)
  between operations  13.2 us (4%)
  starting transfers between devices  5.62 us (2%)
    scatter-add x16, other arithmetic, advance(): return (totals.at[slot_set].add(products * alive_set[:, None, None]), None)  72.9 us
    ppermute x3, waiting for transfers between devices, grow_blocks(): other = lax.ppermute(tiles, axis, [(i, i ^ apart) for i in range(peers)])  62 us
    dot_general x16, matrix products, advance(): jnp.einsum('tij,tjf->tif', tile_set, source, preferred_element_type=jnp.f...  48 us
    reduce_scatter x2, waiting for transfers between devices, reduce_rows(): lax.psum_scatter(spread_sums.reshape(group_count * block_count, tile_size...  45.5 us
    gather x16, local copies, waits for them, and re-layouts, advance(): source = jnp.take(sources, column_set, axis=0)  41.6 us
    all_gather x1, waiting for transfers between devices, body(): gathered = lax.all_gather(local_rows, 'member', axis=0, tiled=True)  39.4 us
  transfers between devices with their start and end apart: 6, of which 6 were waited for; matrix products, arithmetic and copies ran while one was open for 2% of the time, Pallas kernels for 0%

profile of v1, /device:TPU:0, one launch (start us, length us, event | category | flops | bytes accessed | tf_op | source)
XLA Modules:
  0.0 345.1 jit_solution(8583607423105681311)
XLA Ops:
  13.0 39.4 %all-gather.2.cloned.1.call-done = bf16[32,128,128]{2,1,0:T(8,128)(2,1)} async-done(((bf16[4,128,128]{2,1,0:T(8,128)(2,1)}), bf16[32,128,128]{2,1,0:T(8,128)(2,1)}) %all-gather.2.cloned.1.call-update) | async-done | bytes 1048592 | tf_op jit(solution)/shard_map/all_gather | solution.py:99
  52.4 61.8 %while.20 = (s32[]{:T(128)}, f32[8,128,128]{2,1,0:T(8,128)S(1)}, s32[8,32]{1,0:T(8,128)S(1)}, bf16[8,32,128,128]{3,2,1,0:T(8,128)(2,1)}, s32[8,32]{1,0:T(8,128)S...) while((s32[]{:T(128)}, f32[8,128,128]{2,1,0:T(8,128)S(1)}, s32[8,32]{1,0:T(8,128)S(1)}, ...), condition=%wide.region_3.4_spmd, body=%wide.region_1.3_spmd.sunk | while | flops 135792000 | bytes 12589089 | solution.py:47
  52.4 2.9 gather_fusion
  60.2 2.9 gather_fusion
  67.9 2.9 gather_fusion
  75.6 2.9 gather_fusion
  83.4 2.9 gather_fusion
  91.1 2.9 gather_fusion
  98.8 2.9 gather_fusion
  106.6 2.9 gather_fusion
  115.9 20.5 %reduce-scatter.3.cloned.1.call-done = bf16[4,128,128]{2,1,0:T(8,128)(2,1)} async-done(((bf16[16,128,128]{2,1,0:T(8,128)(2,1)}), bf16[4,128,128]{2,1,0:T(8,128)(2,1)}) %reduce-scatter.3.cloned.1.call-update) | async-done | bytes 131088 | tf_op jit(solution)/shard_map/reduce_scatter | solution.py:89
  139.1 6.6 %collective-permute-done = bf16[1,4,128,256]{3,2,1,0:T(8,128)(2,1)S(1)} collective-permute-done((bf16[1,4,128,256]{3,2,1,0:T(8,128)(2,1)S(1)}, bf16[1,4,128,256]{3,2,1,0:T(8,128)(2,1)S(1)}, u32[]{:S(2)}, u32[]{:S(2)}) %collective-permute-start) | collective-permute-done | bytes 262176 | tf_op jit(solution)/shard_map/ppermute | solution.py:18
  147.3 11.3 %collective-permute-done.1 = bf16[2,4,128,256]{3,2,1,0:T(8,128)(2,1)S(1)} collective-permute-done((bf16[2,4,128,256]{3,2,1,0:T(8,128)(2,1)S(1)}, bf16[2,4,128,256]{3,2,1,0:T(8,128)(2,1)S(1)}, u32[]{:S(2)}, u32[]{:S(2)}) %collective-permute-start.1) | collective-permute-done | bytes 524320 | tf_op jit(solution)/shard_map/ppermute | solution.py:18
  161.3 44.1 %collective-permute-done.2 = bf16[4,4,128,256]{3,2,1,0:T(8,128)(2,1)S(1)} collective-permute-done((bf16[4,4,128,256]{3,2,1,0:T(8,128)(2,1)S(1)}, bf16[4,4,128,256]{3,2,1,0:T(8,128)(2,1)S(1)}, u32[]{:S(2)}, u32[]{:S(2)}) %collective-permute-start.2) | collective-permute-done | bytes 1048608 | tf_op jit(solution)/shard_map/ppermute | solution.py:18
  207.1 102.1 %while.21 = (s32[]{:T(128)}, f32[8,128,256]{2,1,0:T(8,128)S(1)}, s32[8,32]{1,0:T(8,128)S(1)}, bf16[8,32,128,128]{3,2,1,0:T(8,128)(2,1)}, s32[8,32]{1,0:T(8,128)S...) while((s32[]{:T(128)}, f32[8,128,256]{2,1,0:T(8,128)S(1)}, s32[8,32]{1,0:T(8,128)S(1)}, ...), condition=%wide.region_7.8_spmd, body=%wide.region_5.7_spmd.sunk | while | flops 271582592 | bytes 24123424 | solution.py:47
  209.5 3.9 %convolution_multiply_fusion.5 = f32[32,128,256]{2,1,0:T(8,128)} fusion(f32[32]{0:T(128)S(1)} %fusion.53, bf16[32,128,256]{2,1,0:T(8,128)(2,1)S(1)} %gather_fusion.1, pred[32]{0:T(512)(128)(4,1)S(1)} %compare_and_fusion.5, bf16[8,32,128,128]{3,2,1,0:T(8,128)(2,1)} %get-tuple-element.256, s32[]{:T(128)} %get-tuple-element.245), kind=kOutput, calls=%fused_computation.24.clone.1 | convolution fusion | flops 270532608 | bytes 7340704 | tf_op jit(solution)/shard_map/while/body/eval_jaxpr/tij,tjf->tif/dot_general | solution.py:43
  213.4 6.4 %scatter_fusion.1 = f32[8,128,256]{2,1,0:T(8,128)S(1)} fusion(f32[8,128,256]{2,1,0:T(8,128)S(1)} %get-tuple-element.246, s32[32]{0:T(128)S(1)} %get-tuple-element.211, f32[32,128,256]{2,1,0:T(8,128)} %convolution_multiply_fusion.5), kind=kCustom, calls=%fused_computation.3.clone.1 | custom fusion | flops 1048576 | bytes 12583040 | tf_op jit(solution)/shard_map/while/body/eval_jaxpr/scatter-add | solution.py:44
  222.2 3.9 %convolution_multiply_fusion.5 = f32[32,128,256]{2,1,0:T(8,128)} fusion(f32[32]{0:T(128)S(1)} %fusion.53, bf16[32,128,256]{2,1,0:T(8,128)(2,1)S(1)} %gather_fusion.1, pred[32]{0:T(512)(128)(4,1)S(1)} %compare_and_fusion.5, bf16[8,32,128,128]{3,2,1,0:T(8,128)(2,1)} %get-tuple-element.256, s32[]{:T(128)} %get-tuple-element.245), kind=kOutput, calls=%fused_computation.24.clone.1 | convolution fusion | flops 270532608 | bytes 7340704 | tf_op jit(solution)/shard_map/while/body/eval_jaxpr/tij,tjf->tif/dot_general | solution.py:43
  226.2 6.4 %scatter_fusion.1 = f32[8,128,256]{2,1,0:T(8,128)S(1)} fusion(f32[8,128,256]{2,1,0:T(8,128)S(1)} %get-tuple-element.246, s32[32]{0:T(128)S(1)} %get-tuple-element.211, f32[32,128,256]{2,1,0:T(8,128)} %convolution_multiply_fusion.5), kind=kCustom, calls=%fused_computation.3.clone.1 | custom fusion | flops 1048576 | bytes 12583040 | tf_op jit(solution)/shard_map/while/body/eval_jaxpr/scatter-add | solution.py:44
  235.0 3.9 %convolution_multiply_fusion.5 = f32[32,128,256]{2,1,0:T(8,128)} fusion(f32[32]{0:T(128)S(1)} %fusion.53, bf16[32,128,256]{2,1,0:T(8,128)(2,1)S(1)} %gather_fusion.1, pred[32]{0:T(512)(128)(4,1)S(1)} %compare_and_fusion.5, bf16[8,32,128,128]{3,2,1,0:T(8,128)(2,1)} %get-tuple-element.256, s32[]{:T(128)} %get-tuple-element.245), kind=kOutput, calls=%fused_computation.24.clone.1 | convolution fusion | flops 270532608 | bytes 7340704 | tf_op jit(solution)/shard_map/while/body/eval_jaxpr/tij,tjf->tif/dot_general | solution.py:43
  238.9 6.5 %scatter_fusion.1 = f32[8,128,256]{2,1,0:T(8,128)S(1)} fusion(f32[8,128,256]{2,1,0:T(8,128)S(1)} %get-tuple-element.246, s32[32]{0:T(128)S(1)} %get-tuple-element.211, f32[32,128,256]{2,1,0:T(8,128)} %convolution_multiply_fusion.5), kind=kCustom, calls=%fused_computation.3.clone.1 | custom fusion | flops 1048576 | bytes 12583040 | tf_op jit(solution)/shard_map/while/body/eval_jaxpr/scatter-add | solution.py:44
  247.7 3.9 %convolution_multiply_fusion.5 = f32[32,128,256]{2,1,0:T(8,128)} fusion(f32[32]{0:T(128)S(1)} %fusion.53, bf16[32,128,256]{2,1,0:T(8,128)(2,1)S(1)} %gather_fusion.1, pred[32]{0:T(512)(128)(4,1)S(1)} %compare_and_fusion.5, bf16[8,32,128,128]{3,2,1,0:T(8,128)(2,1)} %get-tuple-element.256, s32[]{:T(128)} %get-tuple-element.245), kind=kOutput, calls=%fused_computation.24.clone.1 | convolution fusion | flops 270532608 | bytes 7340704 | tf_op jit(solution)/shard_map/while/body/eval_jaxpr/tij,tjf->tif/dot_general | solution.py:43
  251.7 6.5 %scatter_fusion.1 = f32[8,128,256]{2,1,0:T(8,128)S(1)} fusion(f32[8,128,256]{2,1,0:T(8,128)S(1)} %get-tuple-element.246, s32[32]{0:T(128)S(1)} %get-tuple-element.211, f32[32,128,256]{2,1,0:T(8,128)} %convolution_multiply_fusion.5), kind=kCustom, calls=%fused_computation.3.clone.1 | custom fusion | flops 1048576 | bytes 12583040 | tf_op jit(solution)/shard_map/while/body/eval_jaxpr/scatter-add | solution.py:44
  260.5 3.9 %convolution_multiply_fusion.5 = f32[32,128,256]{2,1,0:T(8,128)} fusion(f32[32]{0:T(128)S(1)} %fusion.53, bf16[32,128,256]{2,1,0:T(8,128)(2,1)S(1)} %gather_fusion.1, pred[32]{0:T(512)(128)(4,1)S(1)} %compare_and_fusion.5, bf16[8,32,128,128]{3,2,1,0:T(8,128)(2,1)} %get-tuple-element.256, s32[]{:T(128)} %get-tuple-element.245), kind=kOutput, calls=%fused_computation.24.clone.1 | convolution fusion | flops 270532608 | bytes 7340704 | tf_op jit(solution)/shard_map/while/body/eval_jaxpr/tij,tjf->tif/dot_general | solution.py:43
  264.5 6.4 %scatter_fusion.1 = f32[8,128,256]{2,1,0:T(8,128)S(1)} fusion(f32[8,128,256]{2,1,0:T(8,128)S(1)} %get-tuple-element.246, s32[32]{0:T(128)S(1)} %get-tuple-element.211, f32[32,128,256]{2,1,0:T(8,128)} %convolution_multiply_fusion.5), kind=kCustom, calls=%fused_computation.3.clone.1 | custom fusion | flops 1048576 | bytes 12583040 | tf_op jit(solution)/shard_map/while/body/eval_jaxpr/scatter-add | solution.py:44
  273.3 3.9 %convolution_multiply_fusion.5 = f32[32,128,256]{2,1,0:T(8,128)} fusion(f32[32]{0:T(128)S(1)} %fusion.53, bf16[32,128,256]{2,1,0:T(8,128)(2,1)S(1)} %gather_fusion.1, pred[32]{0:T(512)(128)(4,1)S(1)} %compare_and_fusion.5, bf16[8,32,128,128]{3,2,1,0:T(8,128)(2,1)} %get-tuple-element.256, s32[]{:T(128)} %get-tuple-element.245), kind=kOutput, calls=%fused_computation.24.clone.1 | convolution fusion | flops 270532608 | bytes 7340704 | tf_op jit(solution)/shard_map/while/body/eval_jaxpr/tij,tjf->tif/dot_general | solution.py:43
  277.2 6.4 %scatter_fusion.1 = f32[8,128,256]{2,1,0:T(8,128)S(1)} fusion(f32[8,128,256]{2,1,0:T(8,128)S(1)} %get-tuple-element.246, s32[32]{0:T(128)S(1)} %get-tuple-element.211, f32[32,128,256]{2,1,0:T(8,128)} %convolution_multiply_fusion.5), kind=kCustom, calls=%fused_computation.3.clone.1 | custom fusion | flops 1048576 | bytes 12583040 | tf_op jit(solution)/shard_map/while/body/eval_jaxpr/scatter-add | solution.py:44
  286.0 3.9 %convolution_multiply_fusion.5 = f32[32,128,256]{2,1,0:T(8,128)} fusion(f32[32]{0:T(128)S(1)} %fusion.53, bf16[32,128,256]{2,1,0:T(8,128)(2,1)S(1)} %gather_fusion.1, pred[32]{0:T(512)(128)(4,1)S(1)} %compare_and_fusion.5, bf16[8,32,128,128]{3,2,1,0:T(8,128)(2,1)} %get-tuple-element.256, s32[]{:T(128)} %get-tuple-element.245), kind=kOutput, calls=%fused_computation.24.clone.1 | convolution fusion | flops 270532608 | bytes 7340704 | tf_op jit(solution)/shard_map/while/body/eval_jaxpr/tij,tjf->tif/dot_general | solution.py:43
  290.0 6.5 %scatter_fusion.1 = f32[8,128,256]{2,1,0:T(8,128)S(1)} fusion(f32[8,128,256]{2,1,0:T(8,128)S(1)} %get-tuple-element.246, s32[32]{0:T(128)S(1)} %get-tuple-element.211, f32[32,128,256]{2,1,0:T(8,128)} %convolution_multiply_fusion.5), kind=kCustom, calls=%fused_computation.3.clone.1 | custom fusion | flops 1048576 | bytes 12583040 | tf_op jit(solution)/shard_map/while/body/eval_jaxpr/scatter-add | solution.py:44
  298.8 3.9 %convolution_multiply_fusion.5 = f32[32,128,256]{2,1,0:T(8,128)} fusion(f32[32]{0:T(128)S(1)} %fusion.53, bf16[32,128,256]{2,1,0:T(8,128)(2,1)S(1)} %gather_fusion.1, pred[32]{0:T(512)(128)(4,1)S(1)} %compare_and_fusion.5, bf16[8,32,128,128]{3,2,1,0:T(8,128)(2,1)} %get-tuple-element.256, s32[]{:T(128)} %get-tuple-element.245), kind=kOutput, calls=%fused_computation.24.clone.1 | convolution fusion | flops 270532608 | bytes 7340704 | tf_op jit(solution)/shard_map/while/body/eval_jaxpr/tij,tjf->tif/dot_general | solution.py:43
  302.7 6.5 %scatter_fusion.1 = f32[8,128,256]{2,1,0:T(8,128)S(1)} fusion(f32[8,128,256]{2,1,0:T(8,128)S(1)} %get-tuple-element.246, s32[32]{0:T(128)S(1)} %get-tuple-element.211, f32[32,128,256]{2,1,0:T(8,128)} %convolution_multiply_fusion.5), kind=kCustom, calls=%fused_computation.3.clone.1 | custom fusion | flops 1048576 | bytes 12583040 | tf_op jit(solution)/shard_map/while/body/eval_jaxpr/scatter-add | solution.py:44
  311.7 25.0 %reduce-scatter.5.cloned.1.call-done = bf16[4,128,256]{2,1,0:T(8,128)(2,1)} async-done(((bf16[16,128,256]{2,1,0:T(8,128)(2,1)}), bf16[4,128,256]{2,1,0:T(8,128)(2,1)}) %reduce-scatter.5.cloned.1.call-update) | async-done | bytes 262160 | tf_op jit(solution)/shard_map/reduce_scatter | solution.py:89
  (131 shorter events, 77.5 us)
Async XLA Ops:
  6.5 330.2 %copy-start = (bf16[256,256]{1,0:T(8,128)(2,1)S(1)}, bf16[256,256]{1,0:T(8,128)(2,1)}, u32[]{:S(2)}) copy-start(bf16[256,256]{1,0:T(8,128)(2,1)} %param.22) | copy-start | bytes 393220
  6.5 45.8 %all-gather.2.cloned.1.call-start = ((), (), s32[]{:S(2)}) async-start(), calls=%async_computation.2 | async-start | bytes 1179648 | tf_op jit(solution)/shard_map/all_gather | solution.py:99
  7.3 129.2 %reduce-scatter.3.cloned.1.call-start = ((), (), s32[]{:S(2)}) async-start(), calls=%async_computation.3 | async-start | bytes 655360 | tf_op jit(solution)/shard_map/reduce_scatter | solution.py:89
  114.3 22.2 %copy-start.1 = (bf16[128,256]{1,0:T(8,128)(2,1)S(1)}, bf16[128,256]{1,0:T(8,128)(2,1)}, u32[]{:S(2)}) copy-start(bf16[128,256]{1,0:T(8,128)(2,1)} %param.20) | copy-start | bytes 196612
  114.3 22.1 %copy-start.2 = (f32[256]{0:T(256)S(1)}, f32[256]{0:T(256)}, u32[]{:S(2)}) copy-start(f32[256]{0:T(256)} %param.21) | copy-start | bytes 3076
  115.8 220.9 %reduce-scatter.5.cloned.1.call-start = ((), (), s32[]{:S(2)}) async-start(), calls=%async_computation.4 | async-start | bytes 1310720 | tf_op jit(solution)/shard_map/reduce_scatter | solution.py:89
  137.5 8.1 %collective-permute-start = (bf16[1,4,128,256]{3,2,1,0:T(8,128)(2,1)S(1)}, bf16[1,4,128,256]{3,2,1,0:T(8,128)(2,1)S(1)}, u32[]{:S(2)}, u32[]{:S(2)}) collective-permute-start(bf16[1,4,128,256]{3,2,1,0:T(8,128)(2,1)S(1)} %bitcast.86), channel_id=1, source_target_pairs={{0,1},{1,0},{2,3},{3,2},{4,5},{5,4},{6,7},{7,6},{8,9},{9,8},{10,11... | collective-permute-start | bytes 786440 | tf_op jit(solution)/shard_map/ppermute | solution.py:18
  145.8 12.9 %collective-permute-start.1 = (bf16[2,4,128,256]{3,2,1,0:T(8,128)(2,1)S(1)}, bf16[2,4,128,256]{3,2,1,0:T(8,128)(2,1)S(1)}, u32[]{:S(2)}, u32[]{:S(2)}) collective-permute-start(bf16[2,4,128,256]{3,2,1,0:T(8,128)(2,1)S(1)} %pad_maximum_fusion.2), channel_id=1, source_target_pairs={{0,2},{1,3},{2,0},{3,1},{4,6},{5,7},{6,4},{7,5},{8,10},{9,11},{10,... | collective-permute-start | bytes 1572872 | tf_op jit(solution)/shard_map/ppermute | solution.py:18
  158.8 46.6 %collective-permute-start.2 = (bf16[4,4,128,256]{3,2,1,0:T(8,128)(2,1)S(1)}, bf16[4,4,128,256]{3,2,1,0:T(8,128)(2,1)S(1)}, u32[]{:S(2)}, u32[]{:S(2)}) collective-permute-start(bf16[4,4,128,256]{3,2,1,0:T(8,128)(2,1)S(1)} %pad_maximum_fusion.1), channel_id=1, source_target_pairs={{0,4},{1,5},{2,6},{3,7},{4,0},{5,1},{6,2},{7,3},{8,12},{9,13},{10,... | collective-permute-start | bytes 3145736 | tf_op jit(solution)/shard_map/ppermute | solution.py:18
  310.5 26.2 %copy-start.3 = (f32[256]{0:T(256)S(1)}, f32[256]{0:T(256)}, u32[]{:S(2)}) copy-start(f32[256]{0:T(256)} %param.23) | copy-start | bytes 3076
Sparse Core Ops, SparseCore 0:
  9.5 42.8 all-gather.1
  116.0 20.4 reduce-scatter.2
  311.8 24.8 reduce-scatter.4
